TPU v7x, 32 devices: a whole 2x2x4 slice. The times are simulated.
32 devices in a mesh: grp: 4 (over x, core), vec: 8 (over z, y).
Axes of the slice: x: 2, y: 2, z: 4, core: 2. Of those that a mesh axis runs over, the one named last changes fastest.
Arguments:
- vv_vectors: bfloat16 [1280, 1000, 1000], P(('grp', 'vec')), may hold values from -0.1875 to 0.1875
- oo_vectors: bfloat16 [1280, 100, 100], P(('grp', 'vec')), may hold values from -0.625 to 0.625
- ov_slab: bfloat16 [1280, 1024], P(('grp', 'vec')), may hold values from -0.15625 to 0.15625
- amplitudes: bfloat16 [100, 1000], P('grp'), may hold values from -6 to 6
Outputs:
- sigma_slab: float32 [96000, 1024], P(('grp', 'vec'))
All inputs are finite; a program needn't handle non-finite values.
Results may differ from a plain program's by a relative error of at most 0.0029.
Values may be sent and summed in bfloat16 or wider, within the bound.
A program may use at most 192 MiB of HBM per device.

v0:
```python
import jax
import jax.numpy as jnp
from jax import lax
from jax.sharding import PartitionSpec as P

NV = 1000
I_ROWS = 96


def shards(vv_vectors, oo_vectors, ov_slab, amplitudes):
    amps_all = lax.all_gather(amplitudes, "grp", axis=0, tiled=True)
    window = amps_all[:I_ROWS]
    local_count = vv_vectors.shape[0]
    direct_term = jnp.einsum("ib,pab->pia", window, vv_vectors, preferred_element_type=jnp.float32)
    hole_term = jnp.einsum(
        "pji,ja->pia", oo_vectors[:, :, :I_ROWS], amps_all, preferred_element_type=jnp.float32
    )
    dressed = (direct_term - hole_term).astype(jnp.bfloat16).reshape(local_count, I_ROWS * NV)
    regrouped = lax.all_to_all(dressed, ("grp", "vec"), split_axis=1, concat_axis=0, tiled=True)
    return lax.dot_general(
        regrouped,
        lax.all_gather(ov_slab, ("grp", "vec"), axis=0, tiled=True),
        (((0,), (0,)), ((), ())),
        preferred_element_type=jnp.float32,
    )


def solution(mesh):
    return jax.shard_map(
        shards,
        mesh=mesh,
        in_specs=(
            P(("grp", "vec"), None, None),
            P(("grp", "vec"), None, None),
            P(("grp", "vec"), None),
            P("grp", None),
        ),
        out_specs=P(("grp", "vec"), None),
        check_vma=False,
    )
```

profile of v0, /device:TPU:0, one launch (start us, length us, event | category | flops | bytes accessed | tf_op | source)
XLA Modules:
  0.0 306.0 jit_solution(5627341047217568495)
XLA Ops:
  6.5 7.4 %all-gather = bf16[4,25,1000]{2,1,0:T(8,128)(2,1)S(1)} all-gather(bf16[1,25,1000]{2,1,0:T(8,128)(2,1)} %bitcast.17), channel_id=1, replica_groups=mesh['grp'=4,'vec'=8] {'grp'}, dimensions={0}, use_global_device_ids=true | all-gather | bytes 250000 | tf_op jit(solution)/shard_map/all_gather | solution.py:11
  14.0 0.1 reshape.6
  14.0 0.1 reshape.8
  14.1 0.0 copy-start
  14.1 38.1 %fusion.2 = f32[40,1000,96]{1,2,0:T(8,128)} fusion(bf16[40,1000,1000]{2,1,0:T(8,128)(2,1)} %param.4, bf16[100,1000]{1,0:T(8,128)(2,1)S(1)} %reshape.6), kind=kOutput, calls=%fused_computation.4 | convolution fusion | flops 7680000000 | bytes 95556608 | tf_op jit(solution)/shard_map/ib,pab->pia/dot_general | solution.py:14
  52.2 0.0 copy-done
  52.2 11.0 %fusion = bf16[40,96,1000]{2,1,0:T(8,128)(2,1)} fusion(f32[40,1000,96]{1,2,0:T(8,128)} %fusion.2, bf16[100,1000,1]{1,0,2:T(8,128)(2,1)S(1)} %reshape.8, bf16[40,100,96]{2,0,1:T(8,128)(2,1)S(1)} %bitcast.16), kind=kOutput, calls=%fused_computation.1 | convolution fusion | flops 775680000 | bytes 24008000 | tf_op jit(solution)/shard_map/pji,ja->pia/dot_general | solution.py:15
  63.3 14.6 %all_to_all.14 = bf16[40,32,3000]{2,1,0:T(8,128)(2,1)} reshape(bf16[40,96,1000]{2,1,0:T(8,128)(2,1)} %fusion) | data formatting | bytes 15360000 | tf_op jit(solution)/shard_map/all_to_all | solution.py:19
  77.8 10.8 %copy.9 = bf16[40,32,3000]{2,0,1:T(8,128)(2,1)} copy(bf16[40,32,3000]{2,1,0:T(8,128)(2,1)} %all_to_all.14) | data formatting | bytes 15360000 | tf_op jit(solution)/shard_map/all_to_all | solution.py:19
  88.6 6.0 %all-to-all-start = ((bf16[40,32,3000]{2,0,1:T(8,128)(2,1)}), bf16[40,32,3000]{2,0,1:T(8,128)(2,1)}, u32[]{:S(2)}, u32[]{:S(2)}) async-start(bf16[40,32,3000]{2,0,1:T(8,128)(2,1)} %copy.9), calls=%async_computation | async-start | bytes 15728640 | tf_op jit(solution)/shard_map/all_to_all | solution.py:19
  94.6 0.0 all-gather.3.cloned.1.call-start
  94.7 0.7 all-gather.3.cloned.1.call-update
  95.3 152.7 %all-gather.3.cloned.1.call-done = bf16[1280,1024]{1,0:T(8,128)(2,1)} async-done(((bf16[40,1024]{1,0:T(8,128)(2,1)}), bf16[1280,1024]{1,0:T(8,128)(2,1)}) %all-gather.3.cloned.1.call-update) | async-done | bytes 2621456 | tf_op jit(solution)/shard_map/all_gather | solution.py:22
  248.1 36.4 %all-to-all-done = bf16[40,32,3000]{2,0,1:T(8,128)(2,1)} async-done(((bf16[40,32,3000]{2,0,1:T(8,128)(2,1)}), bf16[40,32,3000]{2,0,1:T(8,128)(2,1)}, u32[]{:S(2)}, u32[]{:S(2)}) %all-to-all-start) | async-done | bytes 7680032 | tf_op jit(solution)/shard_map/all_to_all | solution.py:19
  284.5 14.7 %fusion.3 = f32[3000,1024]{1,0:T(8,128)} fusion(bf16[1280,3000]{1,0:T(8,128)(2,1)} %bitcast.4, bf16[1280,1024]{1,0:T(8,128)(2,1)} %all-gather.3.cloned.1.call-done), kind=kOutput, calls=%fused_computation.5 | convolution fusion | flops 7864320000 | bytes 22589440 | tf_op jit(solution)/shard_map/dot_general | solution.py:20
Async XLA Ops:
  14.1 38.1 %copy-start = (bf16[40,100,100]{2,0,1:T(8,128)(2,1)S(1)}, bf16[40,100,100]{2,0,1:T(8,128)(2,1)}, u32[]{:S(2)}) copy-start(bf16[40,100,100]{2,0,1:T(8,128)(2,1)} %param.5) | copy-start | bytes 2400004
  88.6 195.9 %all-to-all-start = ((bf16[40,32,3000]{2,0,1:T(8,128)(2,1)}), bf16[40,32,3000]{2,0,1:T(8,128)(2,1)}, u32[]{:S(2)}, u32[]{:S(2)}) async-start(bf16[40,32,3000]{2,0,1:T(8,128)(2,1)} %copy.9), calls=%async_computation | async-start | bytes 15728640 | tf_op jit(solution)/shard_map/all_to_all | solution.py:19
  94.6 153.5 %all-gather.3.cloned.1.call-start = ((), (), s32[]{:S(2)}) async-start(), calls=%async_computation.1 | async-start | bytes 2703360 | tf_op jit(solution)/shard_map/all_gather | solution.py:22
Sparse Core Ops, SparseCore 0:
  98.3 149.7 all-gather.2
where the time goes:
time: 307 us; the launch traced here: 306 us
  waiting for transfers between devices  190 us (62%)
  matrix products  63.8 us (21%)
  local copies, waits for them, and re-layouts  25.5 us (8%)
  between operations  13.4 us (4%)
  blocking collectives  7.42 us (2%)
  starting transfers between devices  6.04 us (2%)
    all_gather x1, waiting for transfers between devices, shards(): lax.all_gather(ov_slab, ('grp', 'vec'), axis=0, tiled=True)  153 us
    dot_general x1, matrix products, shards(): jnp.einsum('ib,pab->pia', window, vv_vectors, preferred_element_type=jnp....  38.1 us
    all_to_all x1, waiting for transfers between devices, shards(): lax.all_to_all(dressed, ('grp', 'vec'), split_axis=1, concat_axis=0, tile...  36.4 us
    all_to_all x2, local copies, waits for them, and re-layouts, shards(): lax.all_to_all(dressed, ('grp', 'vec'), split_axis=1, concat_axis=0, tile...  25.3 us
    dot_general x1, matrix products, shards(): lax.dot_general(regrouped, lax.all_gather(ov_slab, ('grp', 'vec'), axis=0...  14.7 us
    dot_general x1, matrix products, shards(): jnp.einsum('pji,ja->pia', oo_vectors[:, :, :I_ROWS], amps_all, preferred_...  11 us
    all_gather x1, blocking collectives, shards(): amps_all = lax.all_gather(amplitudes, 'grp', axis=0, tiled=True)  7.42 us
  transfers between devices with their start and end apart: 2, of which 2 were waited for; matrix products, arithmetic and copies ran while one was open for 0% of the time, Pallas kernels for 0%

commit v1 on v0

v1 whole, which is shorter than its diff:
```python
import functools
import jax
import jax.numpy as jnp
from jax import lax
from jax.experimental import pallas as pl
from jax.experimental.pallas import tpu as pltpu
from jax.sharding import PartitionSpec as P

I_ROWS = 96
CHUNK = 8
SLOTS = 4
MESH = pl.DeviceIdType.MESH


def farthest_first(count):
    return sorted(range(count), key=lambda k: (abs(k - count // 2), k))


def exchange_kernel(
    ng, nv, inner, amps, oo, ov, vv, out, slab, vv_slots, stage, dressed,
    vv_sem, send_sem, recv_sem, own_sem, col_send, col_recv, plane_send, plane_recv, slab_sem,
):
    g = lax.axis_index("grp")
    v = lax.axis_index("vec")
    me = g * nv + v
    local_count, nvirt = vv.shape[0], vv.shape[1]
    chunks = local_count // CHUNK
    per = I_ROWS // (ng * nv)
    outer = nv // inner
    z = v // inner
    y = lax.rem(v, inner)
    offsets = [(dg, dv) for dv in farthest_first(nv) for dg in range(ng) if (dg, dv) != (0, 0)]
    plane = [(dg, dy) for dg in range(ng) for dy in range(inner) if (dg, dy) != (0, 0)]

    def load(p):
        slot = lax.rem(p, SLOTS)
        return pltpu.make_async_copy(vv.at[p], vv_slots.at[slot], vv_sem.at[slot])

    barrier = pltpu.get_barrier_semaphore()
    for dg, dv in offsets:
        pl.semaphore_signal(
            barrier, inc=1, device_id=(lax.rem(g + dg, ng), lax.rem(v + dv, nv)), device_id_type=MESH
        )
    for p in range(SLOTS):
        load(p).start()
    own_slab = pltpu.make_async_copy(ov, slab.at[g, z, y], slab_sem)
    own_slab.start()
    pl.semaphore_wait(barrier, len(offsets))

    def column_copy(dz):
        return pltpu.make_async_remote_copy(
            src_ref=ov,
            dst_ref=slab.at[g, z, y],
            send_sem=col_send.at[dz],
            recv_sem=col_recv.at[dz],
            device_id=(g, lax.rem(z + dz, outer) * inner + y),
            device_id_type=MESH,
        )

    def plane_copy(j):
        dg, dy = plane[j]
        return pltpu.make_async_remote_copy(
            src_ref=slab.at[g, :, y],
            dst_ref=slab.at[g, :, y],
            send_sem=plane_send.at[j],
            recv_sem=plane_recv.at[j],
            device_id=(lax.rem(g + dg, ng), z * inner + lax.rem(y + dy, inner)),
            device_id_type=MESH,
        )

    for dz in range(1, outer):
        column_copy(dz).start()

    @pl.loop(0, chunks)
    def _(c):
        @pl.loop(0, CHUNK)
        def _(k):
            p = c * CHUNK + k
            load(p).wait()
            direct = lax.dot_general(
                amps[0:I_ROWS, :], vv_slots[lax.rem(p, SLOTS)], (((1,), (1,)), ((), ())),
                preferred_element_type=jnp.float32,
            )
            hole = lax.dot_general(
                oo[p, :, 0:I_ROWS], amps[...], (((0,), (0,)), ((), ())), preferred_element_type=jnp.float32
            )
            value = direct - hole
            for t in range(stage.shape[0]):
                lo, hi = t * 128, min(t * 128 + 128, nvirt)
                stage[t, pl.ds(pl.multiple_of(k * I_ROWS, I_ROWS), I_ROWS), 0:hi - lo] = value[:, lo:hi]

            @pl.when(p + SLOTS < local_count)
            def _():
                load(p + SLOTS).start()

        for i in range(I_ROWS):
            for t in range(stage.shape[0]):
                lo, hi = t * 128, min(t * 128 + 128, nvirt)
                rows = stage[t, pl.ds(i, CHUNK, stride=I_ROWS), :]
                dressed[c, i, :, lo:hi] = rows[:, : hi - lo].astype(jnp.bfloat16)

        for j, (dg, dv) in enumerate(offsets):
            to_g = lax.rem(g + dg, ng)
            to_v = lax.rem(v + dv, nv)
            pltpu.make_async_remote_copy(
                src_ref=dressed.at[c, pl.ds((to_g * nv + to_v) * per, per)],
                dst_ref=out.at[:, me * chunks + c],
                send_sem=send_sem,
                recv_sem=recv_sem.at[j],
                device_id=(to_g, to_v),
                device_id_type=MESH,
            ).start()
        pltpu.make_async_copy(
            dressed.at[c, pl.ds(me * per, per)], out.at[:, me * chunks + c], own_sem
        ).start()

        @pl.when(c == 0)
        def _():
            own_slab.wait()
            for dz in range(1, outer):
                column_copy(dz).wait_send()
                column_copy(dz).wait_recv()
            for j in range(len(plane)):
                plane_copy(j).start()

    def block_wait(sem, source):
        ref = out.at[:, pl.ds(source * chunks, chunks)]
        pltpu.make_async_copy(ref, ref, sem).wait()

    for j in range(len(plane)):
        plane_copy(j).wait_send()
        plane_copy(j).wait_recv()
    everything = out.at[:, pl.ds(0, len(offsets) * chunks)]
    pltpu.make_async_copy(everything, everything, send_sem).wait()
    block_wait(own_sem, me)
    for j, (dg, dv) in enumerate(offsets):
        block_wait(recv_sem.at[j], lax.rem(g + ng - dg, ng) * nv + lax.rem(v + nv - dv, nv))


def exchange(ng, nv, vv_vectors, oo_vectors, ov_slab, amps_all):
    local_count, nvirt = vv_vectors.shape[0], vv_vectors.shape[1]
    devices = ng * nv
    inner = 2 if nv % 2 == 0 else 1
    outer = nv // inner
    chunks = local_count // CHUNK
    per = I_ROWS // devices
    lanes = -(-nvirt // 128) * 128
    anywhere = pl.BlockSpec(memory_space=pl.ANY)
    vmem = pl.BlockSpec(memory_space=pltpu.VMEM)
    dma = pltpu.SemaphoreType.DMA
    regrouped, slab = pl.pallas_call(
        functools.partial(exchange_kernel, ng, nv, inner),
        out_shape=(
            jax.ShapeDtypeStruct((per, devices * chunks, CHUNK, nvirt), jnp.bfloat16),
            jax.ShapeDtypeStruct((ng, outer, inner) + ov_slab.shape, jnp.bfloat16),
        ),
        in_specs=[vmem, vmem, anywhere, anywhere],
        out_specs=(anywhere, anywhere),
        scratch_shapes=[
            pltpu.VMEM((SLOTS, nvirt, nvirt), jnp.bfloat16),
            pltpu.VMEM((lanes // 128, CHUNK * I_ROWS, 128), jnp.float32),
            pltpu.VMEM((chunks, I_ROWS, CHUNK, nvirt), jnp.bfloat16),
            dma((SLOTS,)),
            dma,
            dma((devices - 1,)),
            dma,
            dma((outer,)),
            dma((outer,)),
            dma((ng * inner - 1,)),
            dma((ng * inner - 1,)),
            dma,
        ],
        compiler_params=pltpu.CompilerParams(
            collective_id=0, has_side_effects=True, vmem_limit_bytes=48 * 1024 * 1024
        ),
    )(amps_all, oo_vectors, ov_slab, vv_vectors)
    return regrouped.reshape(per, devices * local_count, nvirt), slab.reshape(-1, ov_slab.shape[1])


def plain(vv_vectors, oo_vectors, ov_slab, amps_all):
    local_count, nvirt = vv_vectors.shape[0], vv_vectors.shape[1]
    window = amps_all[:I_ROWS]
    direct_term = jnp.einsum("ib,pab->pia", window, vv_vectors, preferred_element_type=jnp.float32)
    hole_term = jnp.einsum(
        "pji,ja->pia", oo_vectors[:, :, :I_ROWS], amps_all, preferred_element_type=jnp.float32
    )
    dressed = (direct_term - hole_term).astype(jnp.bfloat16).reshape(local_count, I_ROWS * nvirt)
    regrouped = lax.all_to_all(dressed, ("grp", "vec"), split_axis=1, concat_axis=0, tiled=True)
    return lax.dot_general(
        regrouped,
        lax.all_gather(ov_slab, ("grp", "vec"), axis=0, tiled=True),
        (((0,), (0,)), ((), ())),
        preferred_element_type=jnp.float32,
    )


def solution(mesh):
    ng, nv = mesh.shape["grp"], mesh.shape["vec"]

    def shards(vv_vectors, oo_vectors, ov_slab, amplitudes):
        amps_all = lax.all_gather(amplitudes, "grp", axis=0, tiled=True)
        if I_ROWS % (ng * nv) or vv_vectors.shape[0] % CHUNK:
            return plain(vv_vectors, oo_vectors, ov_slab, amps_all)
        regrouped, slab = exchange(ng, nv, vv_vectors, oo_vectors, ov_slab, amps_all)
        sigma = lax.dot_general(
            regrouped, slab, (((1,), (0,)), ((), ())), preferred_element_type=jnp.float32
        )
        return sigma.reshape(-1, slab.shape[1])

    return jax.shard_map(
        shards,
        mesh=mesh,
        in_specs=(
            P(("grp", "vec"), None, None),
            P(("grp", "vec"), None, None),
            P(("grp", "vec"), None),
            P("grp", None),
        ),
        out_specs=P(("grp", "vec"), None),
        check_vma=False,
    )
```

time: 307 us -> 216 us (0.70)
  the two profiles are of different devices: /device:TPU:0 before, /device:TPU:13 now
where the time goes in v1:
time: 216 us
  Pallas kernels  183 us (85%)
  matrix products  13.1 us (6%)
  local copies, waits for them, and re-layouts  12.8 us (6%)
  blocking collectives  6.49 us (3%)
    pallas_call x1, Pallas kernels, exchange(): pl.pallas_call(functools.partial(exchange_kernel, ng, nv, inner), out_sha...  183 us
    dot_general x1, matrix products, shards(): lax.dot_general(regrouped, slab, (((1,), (0,)), ((), ())), preferred_elem...  13.1 us
    reshape x1, local copies, waits for them, and re-layouts, exchange(): regrouped.reshape(per, devices * local_count, nvirt)  10.4 us
    all_gather x1, blocking collectives, shards(): amps_all = lax.all_gather(amplitudes, 'grp', axis=0, tiled=True)  6.49 us

profile of v1, /device:TPU:13, one launch (start us, length us, event | category | flops | bytes accessed | tf_op | source)
XLA Modules:
  0.0 215.6 jit_solution(13636126562516790705)
XLA Ops:
  0.0 6.5 %all-gather = bf16[4,25,1000]{2,1,0:T(8,128)(2,1)S(1)} all-gather(bf16[1,25,1000]{2,1,0:T(8,128)(2,1)} %bitcast.11), channel_id=1, replica_groups=mesh['grp'=4,'vec'=8] {'grp'}, dimensions={0}, use_global_device_ids=true | all-gather | bytes 250000 | tf_op jit(solution)/shard_map/all_gather | solution.py:201
  6.5 0.1 reshape.11.amps
  6.6 1.4 copy.8.oo
  7.9 0.0 copy-start
  8.0 0.9 copy-done
  8.8 183.3 %shard_map.46 = (bf16[3,160,8,1000]{3,2,1,0:T(8,128)(2,1)}, bf16[4,4,2,40,1024]{4,3,2,1,0:T(8,128)(2,1)S(1)}) custom-call(bf16[100,1000]{1,0:T(8,128)(2,1)S(1)} %reshape.11.amps, bf16[40,100,100]{2,1,0:T(8,128)(2,1)S(1)} %copy.8.oo, bf16[40,1024]{1,0:T(8,128)(2,1)S(1)} %copy-done, bf16[40,1000,1000]{2,1,0:T(8,128)(2,1)} %vv.1), custom_call_target="tpu_custom_call" | custom-call | tf_op jit(solution)/shard_map/pallas_call | solution.py:151
  192.1 10.4 %copy.9 = bf16[3,1280,1000]{1,2,0:T(8,128)(2,1)} copy(bf16[3,1280,1000]{2,1,0:T(8,128)(2,1)} %bitcast.9) | data formatting | bytes 15360000 | tf_op jit(solution)/shard_map/reshape | solution.py:177
  202.6 13.1 %fusion = f32[3000,1024]{1,0:T(8,128)} fusion(bf16[3000,1280]{1,0:T(8,128)(2,1)} %bitcast.10, bf16[1280,1024]{1,0:T(8,128)(2,1)S(1)} %bitcast.8), kind=kOutput, calls=%fused_computation | convolution fusion | flops 7864320000 | bytes 22589440 | tf_op jit(solution)/shard_map/dot_general | solution.py:205
Async XLA Ops:
  7.9 0.9 copy-start

commit v2 on v1

v2 whole, which is shorter than its diff:
```python
import functools
import jax
import jax.numpy as jnp
from jax import lax
from jax.experimental import pallas as pl
from jax.experimental.pallas import tpu as pltpu
from jax.sharding import PartitionSpec as P

I_ROWS = 96
CHUNK = 8
SLOTS = 4
COLUMNS = 256
LIMIT_MIB = 26
FINISH_MIB = 8
MESH = pl.DeviceIdType.MESH


def farthest_first(count):
    return sorted(range(count), key=lambda k: (abs(k - count // 2), k))


def exchange_kernel(
    ng, nv, inner, amps, oo, ov, vv, partial, received, slab,
    vv_slots, stage, dressed, gathered, rows_f32, amps_all,
    vv_sem, send_sem, recv_sem, own_sem, col_send, col_recv, plane_send, plane_recv, slab_sem,
    amps_send, amps_recv, amps_own,
):
    g = lax.axis_index("grp")
    v = lax.axis_index("vec")
    me = g * nv + v
    local_count, nvirt = vv.shape[0], vv.shape[1]
    chunks = local_count // CHUNK
    per = I_ROWS // (ng * nv)
    depth = ng * nv * CHUNK
    outer = nv // inner
    z = v // inner
    y = lax.rem(v, inner)
    held = amps.shape[0]
    offsets = [(dg, dv) for dv in farthest_first(nv) for dg in range(ng) if (dg, dv) != (0, 0)]
    plane = [(dg, dy) for dg in range(ng) for dy in range(inner) if (dg, dy) != (0, 0)]

    def load(p):
        slot = lax.rem(p, SLOTS)
        return pltpu.make_async_copy(vv.at[p], vv_slots.at[slot], vv_sem.at[slot])

    barrier = pltpu.get_barrier_semaphore()
    for dg, dv in offsets:
        pl.semaphore_signal(
            barrier, inc=1, device_id=(lax.rem(g + dg, ng), lax.rem(v + dv, nv)), device_id_type=MESH
        )
    for p in range(SLOTS):
        load(p).start()
    slab_here = slab.at[:, g, z, pl.ds(pl.multiple_of(y * CHUNK, CHUNK), CHUNK)]
    own_slab = pltpu.make_async_copy(ov, slab_here, slab_sem)
    own_slab.start()
    own_amps = pltpu.make_async_copy(amps, gathered.at[g], amps_own)
    own_amps.start()
    pl.semaphore_wait(barrier, len(offsets))

    def amps_copy(dg):
        return pltpu.make_async_remote_copy(
            src_ref=amps,
            dst_ref=gathered.at[g],
            send_sem=amps_send.at[dg],
            recv_sem=amps_recv.at[dg],
            device_id=(lax.rem(g + dg, ng), v),
            device_id_type=MESH,
        )

    def column_copy(dz):
        return pltpu.make_async_remote_copy(
            src_ref=ov,
            dst_ref=slab_here,
            send_sem=col_send.at[dz],
            recv_sem=col_recv.at[dz],
            device_id=(g, lax.rem(z + dz, outer) * inner + y),
            device_id_type=MESH,
        )

    def plane_copy(j):
        dg, dy = plane[j]
        column = slab.at[:, g, :, pl.ds(pl.multiple_of(y * CHUNK, CHUNK), CHUNK)]
        return pltpu.make_async_remote_copy(
            src_ref=column,
            dst_ref=column,
            send_sem=plane_send.at[j],
            recv_sem=plane_recv.at[j],
            device_id=(lax.rem(g + dg, ng), z * inner + lax.rem(y + dy, inner)),
            device_id_type=MESH,
        )

    for dg in range(1, ng):
        amps_copy(dg).start()
    for dz in range(1, outer):
        column_copy(dz).start()
    own_amps.wait()
    for dg in range(1, ng):
        amps_copy(dg).wait_send()
        amps_copy(dg).wait_recv()
    for s in range(ng):
        rows_f32[s * held:(s + 1) * held, :] = gathered[s].astype(jnp.float32)
    amps_all[...] = rows_f32[0:ng * held, :].astype(jnp.bfloat16)

    @pl.loop(0, chunks)
    def _(c):
        @pl.loop(0, CHUNK)
        def _(k):
            p = c * CHUNK + k
            load(p).wait()
            direct = lax.dot_general(
                amps_all[0:I_ROWS, :], vv_slots[lax.rem(p, SLOTS)], (((1,), (1,)), ((), ())),
                preferred_element_type=jnp.float32,
            )
            hole = lax.dot_general(
                oo[p, :, 0:I_ROWS], amps_all[...], (((0,), (0,)), ((), ())),
                preferred_element_type=jnp.float32,
            )
            value = direct - hole
            for t in range(stage.shape[0]):
                lo, hi = t * 128, min(t * 128 + 128, nvirt)
                stage[t, pl.ds(pl.multiple_of(k * I_ROWS, I_ROWS), I_ROWS), 0:hi - lo] = value[:, lo:hi]

            @pl.when(p + SLOTS < local_count)
            def _():
                load(p + SLOTS).start()

        for i in range(I_ROWS):
            for t in range(stage.shape[0]):
                lo, hi = t * 128, min(t * 128 + 128, nvirt)
                rows = stage[t, pl.ds(i, CHUNK, stride=I_ROWS), :]
                dressed[c, i, :, lo:hi] = rows[:, : hi - lo].astype(jnp.bfloat16)

        landing = received.at[c, :, pl.ds(pl.multiple_of(me * CHUNK, CHUNK), CHUNK)]
        for dg, dv in offsets:
            to_g = lax.rem(g + dg, ng)
            to_v = lax.rem(v + dv, nv)
            pltpu.make_async_remote_copy(
                src_ref=dressed.at[c, pl.ds((to_g * nv + to_v) * per, per)],
                dst_ref=landing,
                send_sem=send_sem,
                recv_sem=recv_sem.at[c],
                device_id=(to_g, to_v),
                device_id_type=MESH,
            ).start()
        pltpu.make_async_copy(dressed.at[c, pl.ds(me * per, per)], landing, own_sem.at[c]).start()

        @pl.when(c == 0)
        def _():
            own_slab.wait()
            for dz in range(1, outer):
                column_copy(dz).wait_send()
                column_copy(dz).wait_recv()
            for j in range(len(plane)):
                plane_copy(j).start()

    for j in range(len(plane)):
        plane_copy(j).wait_send()
        plane_copy(j).wait_recv()

    def arrived(c):
        others = received.at[c, :, pl.ds(0, depth - CHUNK)]
        pltpu.make_async_copy(others, others, recv_sem.at[c]).wait()
        mine = received.at[c, :, pl.ds(0, CHUNK)]
        pltpu.make_async_copy(mine, mine, own_sem.at[c]).wait()

    partial[...] = jnp.zeros_like(partial)

    @pl.loop(0, chunks - 1)
    def _(c):
        arrived(c)

        @pl.loop(0, per)
        def _(i):
            lhs = received[c, i]
            rhs = slab[c].reshape(depth, slab.shape[-1])
            for lo in range(0, slab.shape[-1], COLUMNS):
                partial[i, :, lo:lo + COLUMNS] += lax.dot_general(
                    lhs, rhs[:, lo:lo + COLUMNS], (((0,), (0,)), ((), ())),
                    preferred_element_type=jnp.float32,
                )

    arrived(chunks - 1)
    sent = received.at[:, :, pl.ds(0, depth - CHUNK)]
    pltpu.make_async_copy(sent, sent, send_sem).wait()


def finish_kernel(partial, received, slab, out):
    i, j = pl.program_id(0), pl.program_id(1)
    columns = pl.ds(pl.multiple_of(j * COLUMNS, COLUMNS), COLUMNS)
    last = received.shape[0] - 1
    rhs = slab[last, :, :, :, columns].reshape(received.shape[2], COLUMNS)
    out[0] = partial[i, :, columns] + lax.dot_general(
        received[last, i], rhs, (((0,), (0,)), ((), ())), preferred_element_type=jnp.float32
    )


def contract(ng, nv, vv_vectors, oo_vectors, ov_slab, amplitudes):
    local_count, nvirt = vv_vectors.shape[0], vv_vectors.shape[1]
    width = ov_slab.shape[1]
    devices = ng * nv
    inner = 2 if nv % 2 == 0 else 1
    outer = nv // inner
    chunks = local_count // CHUNK
    per = I_ROWS // devices
    lanes = -(-nvirt // 128) * 128
    nocc = ng * amplitudes.shape[0]
    anywhere = pl.BlockSpec(memory_space=pl.ANY)
    vmem = pl.BlockSpec(memory_space=pltpu.VMEM)
    dma = pltpu.SemaphoreType.DMA
    partial, received, slab = pl.pallas_call(
        functools.partial(exchange_kernel, ng, nv, inner),
        out_shape=(
            jax.ShapeDtypeStruct((per, nvirt, width), jnp.float32),
            jax.ShapeDtypeStruct((chunks, per, devices * CHUNK, nvirt), jnp.bfloat16),
            jax.ShapeDtypeStruct((chunks, ng, outer, inner * CHUNK, width), jnp.bfloat16),
        ),
        in_specs=[vmem, vmem, vmem, anywhere],
        out_specs=(vmem, vmem, vmem),
        scratch_shapes=[
            pltpu.VMEM((SLOTS, nvirt, nvirt), jnp.bfloat16),
            pltpu.VMEM((lanes // 128, CHUNK * I_ROWS, 128), jnp.float32),
            pltpu.VMEM((chunks, I_ROWS, CHUNK, nvirt), jnp.bfloat16),
            pltpu.VMEM((ng,) + amplitudes.shape, jnp.bfloat16),
            pltpu.VMEM((nocc, nvirt), jnp.float32),
            pltpu.VMEM((nocc, nvirt), jnp.bfloat16),
            dma((SLOTS,)),
            dma,
            dma((chunks,)),
            dma((chunks,)),
            dma((outer,)),
            dma((outer,)),
            dma((ng * inner - 1,)),
            dma((ng * inner - 1,)),
            dma,
            dma((ng,)),
            dma((ng,)),
            dma,
        ],
        compiler_params=pltpu.CompilerParams(
            collective_id=0, has_side_effects=True, vmem_limit_bytes=LIMIT_MIB * 1024 * 1024
        ),
    )(amplitudes, oo_vectors, ov_slab.reshape(chunks, CHUNK, width), vv_vectors)
    return pl.pallas_call(
        finish_kernel,
        out_shape=jax.ShapeDtypeStruct((per, nvirt, width), jnp.float32),
        grid=(per, width // COLUMNS),
        in_specs=[vmem, vmem, vmem],
        out_specs=pl.BlockSpec((1, nvirt, COLUMNS), lambda i, j: (i, 0, j)),
        compiler_params=pltpu.CompilerParams(vmem_limit_bytes=FINISH_MIB * 1024 * 1024),
    )(partial, received, slab).reshape(per * nvirt, width)


def plain(vv_vectors, oo_vectors, ov_slab, amps_all):
    local_count, nvirt = vv_vectors.shape[0], vv_vectors.shape[1]
    window = amps_all[:I_ROWS]
    direct_term = jnp.einsum("ib,pab->pia", window, vv_vectors, preferred_element_type=jnp.float32)
    hole_term = jnp.einsum(
        "pji,ja->pia", oo_vectors[:, :, :I_ROWS], amps_all, preferred_element_type=jnp.float32
    )
    dressed = (direct_term - hole_term).astype(jnp.bfloat16).reshape(local_count, I_ROWS * nvirt)
    regrouped = lax.all_to_all(dressed, ("grp", "vec"), split_axis=1, concat_axis=0, tiled=True)
    return lax.dot_general(
        regrouped,
        lax.all_gather(ov_slab, ("grp", "vec"), axis=0, tiled=True),
        (((0,), (0,)), ((), ())),
        preferred_element_type=jnp.float32,
    )


def solution(mesh):
    ng, nv = mesh.shape["grp"], mesh.shape["vec"]

    def shards(vv_vectors, oo_vectors, ov_slab, amplitudes):
        if I_ROWS % (ng * nv) or vv_vectors.shape[0] % CHUNK or ov_slab.shape[1] % COLUMNS:
            amps_all = lax.all_gather(amplitudes, "grp", axis=0, tiled=True)
            return plain(vv_vectors, oo_vectors, ov_slab, amps_all)
        return contract(ng, nv, vv_vectors, oo_vectors, ov_slab, amplitudes)

    return jax.shard_map(
        shards,
        mesh=mesh,
        in_specs=(
            P(("grp", "vec"), None, None),
            P(("grp", "vec"), None, None),
            P(("grp", "vec"), None),
            P("grp", None),
        ),
        out_specs=P(("grp", "vec"), None),
        check_vma=False,
    )
```

time: 216 us -> 203 us (0.940)
  Pallas kernels: 183 us -> 198 us
  matrix products: 13.1 us -> 0 us
  local copies, waits for them, and re-layouts: 12.8 us -> 3.08 us
  blocking collectives: 6.49 us -> 0 us
    pallas_call x1 -> x2, Pallas kernels: 183 us -> 198 us  [the longest x1 190 us: contract(): pl.pallas_call(functools.partial(exchange_kernel, ng, nv, inner), out_sha...]
    dot_general x1 -> x0, matrix products: 13.1 us -> none  [shards(): lax.dot_general(regrouped, slab, (((1,), (0,)), ((), ())), preferred_elem...]
    reshape x1 -> x0, local copies, waits for them, and re-layouts: 10.4 us -> none  [exchange(): regrouped.reshape(per, devices * local_count, nvirt)]
    all_gather x1 -> x0, blocking collectives: 6.49 us -> none  [shards(): amps_all = lax.all_gather(amplitudes, 'grp', axis=0, tiled=True)]
where the time goes in v2:
time: 203 us; the launch traced here: 201 us
  Pallas kernels  198 us (98%)
  local copies, waits for them, and re-layouts  3.08 us (2%)
    pallas_call x1, Pallas kernels, contract(): pl.pallas_call(functools.partial(exchange_kernel, ng, nv, inner), out_sha...  190 us
    pallas_call x1, Pallas kernels, contract(): pl.pallas_call(finish_kernel, out_shape=jax.ShapeDtypeStruct((per, nvirt,...  8.19 us

profile of v2, /device:TPU:13, one launch (start us, length us, event | category | flops | bytes accessed | tf_op | source)
XLA Modules:
  0.0 200.8 jit_solution(11703884812415792511)
XLA Ops:
  0.0 1.4 copy.5.oo
  1.4 0.0 copy-start
  1.4 0.9 copy-done
  2.3 0.0 copy-start.1
  2.3 0.8 copy-done.1
  3.1 189.5 %shard_map.46 = (f32[3,1000,1024]{2,1,0:T(8,128)S(1)}, bf16[5,3,256,1000]{3,2,1,0:T(8,128)(2,1)S(1)}, bf16[5,4,4,16,1024]{4,3,2,1,0:T(8,128)(2,1)S(1)}) custom-call(bf16[25,1000]{1,0:T(8,128)(2,1)S(1)} %copy-done.1, bf16[40,100,100]{2,1,0:T(8,128)(2,1)S(1)} %copy.5.oo, bf16[5,8,1024]{2,1,0:T(8,128)(2,1)S(1)} %bitcast.2, bf16[40,1000,1000]{2,1,0:T(8,128)(2,1)} %vv.1), custom_call_target="tpu_custom_call" | custom-call | tf_op jit(solution)/shard_map/pallas_call | solution.py:210
  192.6 8.2 %shard_map.47 = f32[3,1000,1024]{2,1,0:T(8,128)} custom-call(f32[3,1000,1024]{2,1,0:T(8,128)S(1)} %get-tuple-element.8.partial, bf16[5,3,256,1000]{3,2,1,0:T(8,128)(2,1)S(1)} %get-tuple-element.9.received, bf16[5,4,4,16,1024]{4,3,2,1,0:T(8,128)(2,1)S(1)} %get-tuple-element.10.slab), custom_call_target="tpu_custom_call" | custom-call | tf_op jit(solution)/shard_map/pallas_call | solution.py:243
Async XLA Ops:
  1.4 0.9 copy-start
  2.3 0.8 copy-start.1

commit v3 on v2

--- a/solution.py
+++ b/solution.py
@@ -10,6 +10,7 @@
 CHUNK = 8
 SLOTS = 4
 COLUMNS = 256
+FINISH_COLUMNS = 512
 LIMIT_MIB = 26
 FINISH_MIB = 8
 MESH = pl.DeviceIdType.MESH
@@ -124,16 +125,20 @@
             def _():
                 load(p + SLOTS).start()
 
-        for i in range(I_ROWS):
-            for t in range(stage.shape[0]):
-                lo, hi = t * 128, min(t * 128 + 128, nvirt)
-                rows = stage[t, pl.ds(i, CHUNK, stride=I_ROWS), :]
-                dressed[c, i, :, lo:hi] = rows[:, : hi - lo].astype(jnp.bfloat16)
-
         landing = received.at[c, :, pl.ds(pl.multiple_of(me * CHUNK, CHUNK), CHUNK)]
-        for dg, dv in offsets:
-            to_g = lax.rem(g + dg, ng)
-            to_v = lax.rem(v + dv, nv)
+
+        def owner(dv, dg):
+            return lax.rem(g + dg, ng), lax.rem(v + nv + dv * (1 - 2 * lax.rem(g, 2)), nv)
+
+        def regroup(first):
+            for i in range(per):
+                for t in range(stage.shape[0]):
+                    lo, hi = t * 128, min(t * 128 + 128, nvirt)
+                    rows = stage[t, pl.ds(first + i, CHUNK, stride=I_ROWS), :]
+                    dressed[c, first + i, :, lo:hi] = rows[:, : hi - lo].astype(jnp.bfloat16)
+
+        def send(dv, dg):
+            to_g, to_v = owner(dv, dg)
             pltpu.make_async_remote_copy(
                 src_ref=dressed.at[c, pl.ds((to_g * nv + to_v) * per, per)],
                 dst_ref=landing,
@@ -142,6 +147,16 @@
                 device_id=(to_g, to_v),
                 device_id_type=MESH,
             ).start()
+
+        order = [(dv, dg) for dv in range(1, nv) for dg in range(ng)] + [(0, dg) for dg in range(1, ng)]
+        for at, step in enumerate(order):
+            to_g, to_v = owner(*step)
+            regroup((to_g * nv + to_v) * per)
+            if at >= 2:
+                send(*order[at - 2])
+        regroup(me * per)
+        send(*order[-2])
+        send(*order[-1])
         pltpu.make_async_copy(dressed.at[c, pl.ds(me * per, per)], landing, own_sem.at[c]).start()
 
         @pl.when(c == 0)
@@ -186,9 +201,9 @@
 
 def finish_kernel(partial, received, slab, out):
     i, j = pl.program_id(0), pl.program_id(1)
-    columns = pl.ds(pl.multiple_of(j * COLUMNS, COLUMNS), COLUMNS)
+    columns = pl.ds(pl.multiple_of(j * FINISH_COLUMNS, FINISH_COLUMNS), FINISH_COLUMNS)
     last = received.shape[0] - 1
-    rhs = slab[last, :, :, :, columns].reshape(received.shape[2], COLUMNS)
+    rhs = slab[last, :, :, :, columns].reshape(received.shape[2], FINISH_COLUMNS)
     out[0] = partial[i, :, columns] + lax.dot_general(
         received[last, i], rhs, (((0,), (0,)), ((), ())), preferred_element_type=jnp.float32
     )
@@ -204,7 +219,7 @@
     per = I_ROWS // devices
     lanes = -(-nvirt // 128) * 128
     nocc = ng * amplitudes.shape[0]
-    anywhere = pl.BlockSpec(memory_space=pl.ANY)
+    hbm = pl.BlockSpec(memory_space=pltpu.HBM)
     vmem = pl.BlockSpec(memory_space=pltpu.VMEM)
     dma = pltpu.SemaphoreType.DMA
     partial, received, slab = pl.pallas_call(
@@ -214,7 +229,7 @@
             jax.ShapeDtypeStruct((chunks, per, devices * CHUNK, nvirt), jnp.bfloat16),
             jax.ShapeDtypeStruct((chunks, ng, outer, inner * CHUNK, width), jnp.bfloat16),
         ),
-        in_specs=[vmem, vmem, vmem, anywhere],
+        in_specs=[hbm, vmem, hbm, hbm],
         out_specs=(vmem, vmem, vmem),
         scratch_shapes=[
             pltpu.VMEM((SLOTS, nvirt, nvirt), jnp.bfloat16),
@@ -243,9 +258,9 @@
     return pl.pallas_call(
         finish_kernel,
         out_shape=jax.ShapeDtypeStruct((per, nvirt, width), jnp.float32),
-        grid=(per, width // COLUMNS),
+        grid=(per, width // FINISH_COLUMNS),
         in_specs=[vmem, vmem, vmem],
-        out_specs=pl.BlockSpec((1, nvirt, COLUMNS), lambda i, j: (i, 0, j)),
+        out_specs=pl.BlockSpec((1, nvirt, FINISH_COLUMNS), lambda i, j: (i, 0, j)),
         compiler_params=pltpu.CompilerParams(vmem_limit_bytes=FINISH_MIB * 1024 * 1024),
     )(partial, received, slab).reshape(per * nvirt, width)
 
@@ -271,7 +286,7 @@
     ng, nv = mesh.shape["grp"], mesh.shape["vec"]
 
     def shards(vv_vectors, oo_vectors, ov_slab, amplitudes):
-        if I_ROWS % (ng * nv) or vv_vectors.shape[0] % CHUNK or ov_slab.shape[1] % COLUMNS:
+        if I_ROWS % (ng * nv) or vv_vectors.shape[0] % CHUNK or ov_slab.shape[1] % FINISH_COLUMNS:
             amps_all = lax.all_gather(amplitudes, "grp", axis=0, tiled=True)
             return plain(vv_vectors, oo_vectors, ov_slab, amps_all)
         return contract(ng, nv, vv_vectors, oo_vectors, ov_slab, amplitudes)

time: 203 us -> 198 us (0.975)
  Pallas kernels: 198 us -> 193 us
    pallas_call x1, Pallas kernels: 190 us -> 187 us  [contract(): pl.pallas_call(functools.partial(exchange_kernel, ng, nv, inner), out_sha...]
    pallas_call x1, Pallas kernels: 8.19 us -> 6.01 us  [contract(): pl.pallas_call(finish_kernel, out_shape=jax.ShapeDtypeStruct((per, nvirt,...]
where the time goes in v3:
time: 198 us; the launch traced here: 196 us
  Pallas kernels  193 us (97%)
  local copies, waits for them, and re-layouts  3.08 us (2%)
    pallas_call x1, Pallas kernels, contract(): pl.pallas_call(functools.partial(exchange_kernel, ng, nv, inner), out_sha...  187 us
    pallas_call x1, Pallas kernels, contract(): pl.pallas_call(finish_kernel, out_shape=jax.ShapeDtypeStruct((per, nvirt,...  6.01 us

profile of v3, /device:TPU:13, one launch (start us, length us, event | category | flops | bytes accessed | tf_op | source)
XLA Modules:
  0.0 195.7 jit_solution(15429008247866676013)
XLA Ops:
  0.0 1.4 copy.5.oo
  1.4 0.0 copy-start
  1.4 0.9 copy-done
  2.3 0.0 copy-start.1
  2.3 0.8 copy-done.1
  3.1 186.6 %shard_map.46 = (f32[3,1000,1024]{2,1,0:T(8,128)S(1)}, bf16[5,3,256,1000]{3,2,1,0:T(8,128)(2,1)S(1)}, bf16[5,4,4,16,1024]{4,3,2,1,0:T(8,128)(2,1)S(1)}) custom-call(bf16[25,1000]{1,0:T(8,128)(2,1)S(1)} %copy-done.1, bf16[40,100,100]{2,1,0:T(8,128)(2,1)S(1)} %copy.5.oo, bf16[5,8,1024]{2,1,0:T(8,128)(2,1)S(1)} %bitcast.2, bf16[40,1000,1000]{2,1,0:T(8,128)(2,1)} %vv.1), custom_call_target="tpu_custom_call" | custom-call | tf_op jit(solution)/shard_map/pallas_call | solution.py:225
  189.7 6.0 %shard_map.47 = f32[3,1000,1024]{2,1,0:T(8,128)} custom-call(f32[3,1000,1024]{2,1,0:T(8,128)S(1)} %get-tuple-element.8.partial, bf16[5,3,256,1000]{3,2,1,0:T(8,128)(2,1)S(1)} %get-tuple-element.9.received, bf16[5,4,4,16,1024]{4,3,2,1,0:T(8,128)(2,1)S(1)} %get-tuple-element.10.slab), custom_call_target="tpu_custom_call" | custom-call | tf_op jit(solution)/shard_map/pallas_call | solution.py:258
Async XLA Ops:
  1.4 0.9 copy-start
  2.3 0.8 copy-start.1
